TPU v7x, 32 devices: a whole 2x2x4 slice. The times are simulated.
32 devices in a mesh: leaf: 8 (over y, x, core), loop: 4 (over z).
Axes of the slice: x: 2, y: 2, z: 4, core: 2. Of those that a mesh axis runs over, the one named last changes fastest.
Arguments:
- jacobian_t: bfloat16 [4, 8192, 512], P('loop', 'leaf'), may hold values from -6 to 6
- leaf_block: bfloat16 [4, 8192, 1024], P('loop', 'leaf'), may hold values from -0.1875 to 0.1875
- left_basis: bfloat16 [4, 8192, 128], P('loop', 'leaf'), may hold values from -0.5 to 0.5
- right_basis: bfloat16 [4, 8192, 128], P('loop', 'leaf'), may hold values from -0.1875 to 0.1875
- couplings: bfloat16 [4, 24, 128, 128], P('loop', 'leaf'), may hold values from -0.5 to 0.5
- group_coupling: bfloat16 [4, 16, 128, 128], P('loop', 'leaf'), may hold values from -0.5 to 0.5
- obs_order: int32 [512], replicated, may hold values from 0 to 511, each once
Outputs:
- cross_cov: bfloat16 [4, 8192, 512], P('loop', 'leaf')
- projected: float32 [512, 512], P('leaf')
Inputs may be any that keep to these rules, and one draw needn't show every extreme that they name: `obs_order`: each observation 0 to 511 appears exactly once.
All inputs are finite; a program needn't handle non-finite values.
Results may differ from a plain program's by a relative error of at most 0.005.
Values sent between devices are 32-bit elements; how exact they have to be, the bound alone decides.
A program may use at most 64 MiB of HBM per device.

v0:
```python
import jax
import jax.numpy as jnp
from jax import lax
from jax.sharding import PartitionSpec as P


def partner(value, axis, stride):
    mask = 2**stride
    pairs = [(source, source ^ mask) for source in range(lax.axis_size(axis))]
    return lax.ppermute(value, axis, pairs)


def from_behind(shard, axis, by):
    devices = lax.axis_size(axis)
    return lax.ppermute(shard, axis, [(i, (i + by) % devices) for i in range(devices)])


def body(jacobian_t, leaf_block, left_basis, right_basis, couplings, group_coupling, obs_order):
    highest = lax.Precision.HIGHEST
    field = jacobian_t[0]
    block = leaf_block[0]
    lefts = left_basis[0]
    rights = right_basis[0]
    coupled = couplings[0].astype(jnp.float32)
    neighbour = group_coupling[0].astype(jnp.float32)
    coef = lax.dot_general(
        rights, field, (((0,), (0,)), ((), ())), preferred_element_type=jnp.float32
    )
    levels = lax.axis_size("leaf").bit_length() - 1
    total = coef
    mixed = jnp.zeros_like(coef)
    for level in range(levels):
        other = partner(total, "leaf", level)
        mixed = mixed + jnp.dot(coupled[level], other, precision=highest)
        total = total + other
    before = from_behind(total, "loop", 1)
    after = from_behind(total, "loop", -1)
    mixed = mixed + jnp.dot(neighbour[0], before, precision=highest)
    mixed = mixed + jnp.dot(neighbour[1], after, precision=highest)
    mixed = mixed.astype(jnp.bfloat16)
    near = jnp.dot(block, field, preferred_element_type=jnp.float32)
    far = jnp.dot(lefts, mixed, preferred_element_type=jnp.float32)
    cross = (near + far).astype(jnp.bfloat16)
    partial_value = lax.dot_general(
        field, cross, (((0,), (0,)), ((), ())), preferred_element_type=jnp.float32
    )
    ordered = partial_value[obs_order]
    mine = lax.psum_scatter(ordered, "leaf", scatter_dimension=0, tiled=True)
    projected = lax.psum(mine, "loop")
    return (cross[None], projected)


def solution(mesh):
    in_specs = (
        P("loop", "leaf", None),
        P("loop", "leaf", None),
        P("loop", "leaf", None),
        P("loop", "leaf", None),
        P("loop", "leaf", None, None),
        P("loop", "leaf", None, None),
        P(),
    )
    out_specs = (P("loop", "leaf", None), P("leaf", None))
    return jax.shard_map(body, mesh=mesh, in_specs=in_specs, out_specs=out_specs, check_vma=False)
```

profile of v0, /device:TPU:0, one launch (start us, length us, event | category | flops | bytes accessed | tf_op | source)
XLA Modules:
  0.0 131.8 jit_solution(6118895068990609260)
XLA Ops:
  7.2 1.8 %fusion.8 = f32[128,512]{1,0:T(8,128)S(1)} fusion(bf16[1,1024,512]{2,1,0:T(8,128)(2,1)} %param.7, bf16[1,1024,128]{2,1,0:T(8,128)(2,1)} %param.10), kind=kOutput, calls=%fused_computation.12 | convolution fusion | flops 134217728 | bytes 1572864 | tf_op jit(solution)/shard_map/dot_general | solution.py:26
  9.0 0.6 collective-permute-start
  9.6 1.2 collective-permute-done
  10.8 2.9 %collective-permute-start.1 = (f32[128,512]{1,0:T(8,128)S(1)}, f32[128,512]{1,0:T(8,128)S(1)}, u32[]{:S(2)}, u32[]{:S(2)}) collective-permute-start(f32[128,512]{1,0:T(8,128)S(1)} %add.40), channel_id=1, source_target_pairs={{0,8},{4,12},{8,0},{12,4},{16,24},{20,28},{24,16},{28,20},{1,9},{5... | collective-permute-start | bytes 786440 | tf_op jit(solution)/shard_map/ppermute | solution.py:10
  13.7 6.6 %collective-permute-done.1 = f32[128,512]{1,0:T(8,128)S(1)} collective-permute-done((f32[128,512]{1,0:T(8,128)S(1)}, f32[128,512]{1,0:T(8,128)S(1)}, u32[]{:S(2)}, u32[]{:S(2)}) %collective-permute-start.1) | collective-permute-done | bytes 262176 | tf_op jit(solution)/shard_map/ppermute | solution.py:10
  20.4 1.8 %collective-permute-start.2 = (f32[128,512]{1,0:T(8,128)S(1)}, f32[128,512]{1,0:T(8,128)S(1)}, u32[]{:S(2)}, u32[]{:S(2)}) collective-permute-start(f32[128,512]{1,0:T(8,128)S(1)} %add.42), channel_id=1, source_target_pairs={{0,16},{4,20},{8,24},{12,28},{16,0},{20,4},{24,8},{28,12},{1,17},{... | collective-permute-start | bytes 786440 | tf_op jit(solution)/shard_map/ppermute | solution.py:10
  22.2 1.2 fusion.1
  23.5 4.7 %collective-permute-done.2 = f32[128,512]{1,0:T(8,128)S(1)} collective-permute-done((f32[128,512]{1,0:T(8,128)S(1)}, f32[128,512]{1,0:T(8,128)S(1)}, u32[]{:S(2)}, u32[]{:S(2)}) %collective-permute-start.2) | collective-permute-done | bytes 262176 | tf_op jit(solution)/shard_map/ppermute | solution.py:10
  28.3 3.6 %collective-permute-start.4 = (f32[128,512]{1,0:T(8,128)S(1)}, f32[128,512]{1,0:T(8,128)S(1)}, u32[]{:S(2)}, u32[]{:S(2)}) collective-permute-start(f32[128,512]{1,0:T(8,128)S(1)} %add.44), channel_id=1, source_target_pairs={{0,3},{1,0},{2,1},{3,2},{4,7},{5,4},{6,5},{7,6},{8,11},{9,8},{10,9... | collective-permute-start | bytes 786440 | tf_op jit(solution)/shard_map/ppermute | solution.py:15
  31.9 0.4 fusion.19
  32.4 0.4 fusion.17
  32.7 5.8 %collective-permute-done.4 = f32[128,512]{1,0:T(8,128)S(1)} collective-permute-done((f32[128,512]{1,0:T(8,128)S(1)}, f32[128,512]{1,0:T(8,128)S(1)}, u32[]{:S(2)}, u32[]{:S(2)}) %collective-permute-start.4) | collective-permute-done | bytes 262176 | tf_op jit(solution)/shard_map/ppermute | solution.py:15
  38.6 0.4 fusion.13
  39.0 3.6 %collective-permute-done.3 = f32[128,512]{1,0:T(8,128)S(1)} collective-permute-done((f32[128,512]{1,0:T(8,128)S(1)}, f32[128,512]{1,0:T(8,128)S(1)}, u32[]{:S(2)}, u32[]{:S(2)}) %collective-permute-start.3) | collective-permute-done | bytes 262176 | tf_op jit(solution)/shard_map/ppermute | solution.py:15
  42.6 0.4 fusion.15
  43.0 0.4 fusion.6
  43.4 0.4 fusion
  43.8 1.0 copy-done.1
  44.8 1.7 %convolution_bitcast_fusion = f32[512,512]{0,1:T(8,128)} fusion(bf16[1024,512]{1,0:T(8,128)(2,1)S(1)} %fusion, bf16[1,1024,512]{2,1,0:T(8,128)(2,1)S(1)} %copy-done.2), kind=kOutput, calls=%fused_computation.5 | convolution fusion | flops 536870912 | bytes 3145728 | tf_op jit(solution)/shard_map/dot_general | solution.py:44
  46.5 1.6 %copy.10 = f32[512,512]{1,0:T(8,128)S(1)} copy(f32[512,512]{0,1:T(8,128)} %convolution_bitcast_fusion) | data formatting | bytes 2097152 | tf_op jit(solution)/shard_map/dot_general | solution.py:44
  48.1 2.3 %gather_fusion = f32[512,512]{1,0:T(8,128)} fusion(f32[512,512]{1,0:T(8,128)S(1)} %copy.10, s32[1024]{0:T(1024)S(1)} %pad_clamp_fusion), kind=kCustom, calls=%fused_computation | custom fusion | bytes 2099200 | tf_op jit(solution)/shard_map/gather | solution.py:47
  50.5 35.9 %reduce-scatter.2.cloned.1.call-done = f32[64,512]{1,0:T(8,128)} async-done(((f32[512,512]{1,0:T(8,128)}), f32[64,512]{1,0:T(8,128)}) %reduce-scatter.2.cloned.1.call-update) | async-done | bytes 131088 | tf_op jit(solution)/shard_map/reduce_scatter | solution.py:48
  86.4 37.0 %all-reduce.2.cloned.1.call-done = f32[64,512]{1,0:T(8,128)} async-done(((f32[64,512]{1,0:T(8,128)}), f32[64,512]{1,0:T(8,128)}) %all-reduce.2.cloned.1.call-update) | async-done | bytes 131088 | tf_op jit(solution)/shard_map/psum | solution.py:49
  123.4 1.6 %copy.13 = f32[64,512]{1,0:T(8,128)} copy(f32[64,512]{1,0:T(8,128)} %all-reduce.2.cloned.1.call-done) | data formatting | bytes 262144
  (23 shorter events, 0.3 us)
Async XLA Ops:
  7.2 15.1 %copy-start = (bf16[1,1024,1024]{2,1,0:T(8,128)(2,1)S(1)}, bf16[1,1024,1024]{2,1,0:T(8,128)(2,1)}, u32[]{:S(2)}) copy-start(bf16[1,1024,1024]{2,1,0:T(8,128)(2,1)} %param.8) | copy-start | bytes 6291460
  7.2 15.0 %copy-start.2 = (bf16[1,1024,512]{2,1,0:T(8,128)(2,1)S(1)}, bf16[1,1024,512]{2,1,0:T(8,128)(2,1)}, u32[]{:S(2)}) copy-start(bf16[1,1024,512]{2,1,0:T(8,128)(2,1)} %param.7) | copy-start | bytes 3145732
  7.2 6.5 %copy-start.6 = (s32[512]{0:T(512)S(1)}, s32[512]{0:T(512)}, u32[]{:S(2)}) copy-start(s32[512]{0:T(512)} %param.13) | copy-start | bytes 6148
  7.2 79.2 %reduce-scatter.2.cloned.1.call-start = ((), (), s32[]{:S(2)}) async-start(), calls=%async_computation.1 | async-start | bytes 1179648 | tf_op jit(solution)/shard_map/reduce_scatter | solution.py:48
  9.0 1.7 %collective-permute-start = (f32[128,512]{1,0:T(8,128)S(1)}, f32[128,512]{1,0:T(8,128)S(1)}, u32[]{:S(2)}, u32[]{:S(2)}) collective-permute-start(f32[128,512]{1,0:T(8,128)S(1)} %fusion.8), channel_id=1, source_target_pairs={{0,4},{4,0},{8,12},{12,8},{16,20},{20,16},{24,28},{28,24},{1,5},{5... | collective-permute-start | bytes 786440 | tf_op jit(solution)/shard_map/ppermute | solution.py:10
  10.8 9.5 %collective-permute-start.1 = (f32[128,512]{1,0:T(8,128)S(1)}, f32[128,512]{1,0:T(8,128)S(1)}, u32[]{:S(2)}, u32[]{:S(2)}) collective-permute-start(f32[128,512]{1,0:T(8,128)S(1)} %add.40), channel_id=1, source_target_pairs={{0,8},{4,12},{8,0},{12,4},{16,24},{20,28},{24,16},{28,20},{1,9},{5... | collective-permute-start | bytes 786440 | tf_op jit(solution)/shard_map/ppermute | solution.py:10
  20.4 11.5 %copy-start.4 = (bf16[1,3,128,128]{3,2,1,0:T(8,128)(2,1)S(1)}, bf16[1,3,128,128]{3,2,1,0:T(8,128)(2,1)}, u32[]{:S(2)}) copy-start(bf16[1,3,128,128]{3,2,1,0:T(8,128)(2,1)} %param.11) | copy-start | bytes 294916
  20.4 18.2 %copy-start.5 = (bf16[1,2,128,128]{3,2,1,0:T(8,128)(2,1)S(1)}, bf16[1,2,128,128]{3,2,1,0:T(8,128)(2,1)}, u32[]{:S(2)}) copy-start(bf16[1,2,128,128]{3,2,1,0:T(8,128)(2,1)} %param.12) | copy-start | bytes 196612
  20.4 7.8 %collective-permute-start.2 = (f32[128,512]{1,0:T(8,128)S(1)}, f32[128,512]{1,0:T(8,128)S(1)}, u32[]{:S(2)}, u32[]{:S(2)}) collective-permute-start(f32[128,512]{1,0:T(8,128)S(1)} %add.42), channel_id=1, source_target_pairs={{0,16},{4,20},{8,24},{12,28},{16,0},{20,4},{24,8},{28,12},{1,17},{... | collective-permute-start | bytes 786440 | tf_op jit(solution)/shard_map/ppermute | solution.py:10
  23.5 19.9 %copy-start.3 = (bf16[1,1024,128]{2,1,0:T(8,128)(2,1)S(1)}, bf16[1,1024,128]{2,1,0:T(8,128)(2,1)}, u32[]{:S(2)}) copy-start(bf16[1,1024,128]{2,1,0:T(8,128)(2,1)} %param.9) | copy-start | bytes 786436
  28.3 10.3 %collective-permute-start.4 = (f32[128,512]{1,0:T(8,128)S(1)}, f32[128,512]{1,0:T(8,128)S(1)}, u32[]{:S(2)}, u32[]{:S(2)}) collective-permute-start(f32[128,512]{1,0:T(8,128)S(1)} %add.44), channel_id=1, source_target_pairs={{0,3},{1,0},{2,1},{3,2},{4,7},{5,4},{6,5},{7,6},{8,11},{9,8},{10,9... | collective-permute-start | bytes 786440 | tf_op jit(solution)/shard_map/ppermute | solution.py:15
  32.3 10.3 %collective-permute-start.3 = (f32[128,512]{1,0:T(8,128)S(1)}, f32[128,512]{1,0:T(8,128)S(1)}, u32[]{:S(2)}, u32[]{:S(2)}) collective-permute-start(f32[128,512]{1,0:T(8,128)S(1)} %add.44), channel_id=1, source_target_pairs={{0,1},{1,2},{2,3},{3,0},{4,5},{5,6},{6,7},{7,4},{8,9},{9,10},{10,1... | collective-permute-start | bytes 786440 | tf_op jit(solution)/shard_map/ppermute | solution.py:15
  43.8 1.0 copy-start.1
  50.4 72.9 %all-reduce.2.cloned.1.call-start = ((), (), s32[]{:S(2)}) async-start(), calls=%async_computation.2 | async-start | bytes 262144 | tf_op jit(solution)/shard_map/psum | solution.py:49
Sparse Core Ops, SparseCore 0:
  50.5 35.7 reduce-scatter.1
  88.7 34.6 all-reduce.1
where the time goes:
time: 132 us
  waiting for transfers between devices  94.8 us (72%)
  between operations  14.2 us (11%)
  starting transfers between devices  9.07 us (7%)
  matrix products  7.13 us (5%)
  local copies, waits for them, and re-layouts  6.45 us (5%)
    psum x1, waiting for transfers between devices, body(): projected = lax.psum(mine, 'loop')  37 us
    reduce_scatter x1, waiting for transfers between devices, body(): mine = lax.psum_scatter(ordered, 'leaf', scatter_dimension=0, tiled=True)  35.9 us
    ppermute x3, waiting for transfers between devices, partner(): return lax.ppermute(value, axis, pairs)  12.5 us
    ppermute x2, waiting for transfers between devices, from_behind(): lax.ppermute(shard, axis, [(i, (i + by) % devices) for i in range(devices)])  9.41 us
    ppermute x3, starting transfers between devices, partner(): return lax.ppermute(value, axis, pairs)  5.31 us
    ppermute x2, starting transfers between devices, from_behind(): lax.ppermute(shard, axis, [(i, (i + by) % devices) for i in range(devices)])  3.68 us
  transfers between devices with their start and end apart: 7, of which 7 were waited for; matrix products, arithmetic and copies ran while one was open for 2% of the time, Pallas kernels for 0%

commit v1 on v0

--- a/solution.py
+++ b/solution.py
@@ -46,7 +46,7 @@
     )
     ordered = partial_value[obs_order]
     mine = lax.psum_scatter(ordered, "leaf", scatter_dimension=0, tiled=True)
-    projected = lax.psum(mine, "loop")
+    projected = jnp.sum(lax.all_gather(mine, "loop"), axis=0)
     return (cross[None], projected)
 
 

time: 132 us -> 110 us (0.83)
  waiting for transfers between devices: 94.8 us -> 57.9 us
  blocking collectives: 0 us -> 15.6 us
  local copies, waits for them, and re-layouts: 6.45 us -> 4.87 us
    psum x1 -> x0, waiting for transfers between devices: 37 us -> none  [body(): projected = lax.psum(mine, 'loop')]
    all_gather x0 -> x1, blocking collectives: none -> 15.6 us  [body(): projected = jnp.sum(lax.all_gather(mine, 'loop'), axis=0)]
    unnamed x15 -> x14, local copies, waits for them, and re-layouts: 2.57 us -> 1 us
  transfers between devices with their start and end apart: 7 -> 6, of which waited for: 7 -> 6; matrix products, arithmetic and copies ran while one was open for 2% -> 2% of each run, Pallas kernels for 0% -> 0%
where the time goes in v1:
time: 110 us; the launch traced here: 109 us
  waiting for transfers between devices  57.9 us (53%)
  blocking collectives  15.6 us (14%)
  between operations  14.2 us (13%)
  starting transfers between devices  9.03 us (8%)
  matrix products  7.1 us (6%)
  local copies, waits for them, and re-layouts  4.87 us (4%)
    reduce_scatter x1, waiting for transfers between devices, body(): mine = lax.psum_scatter(ordered, 'leaf', scatter_dimension=0, tiled=True)  36 us
    all_gather x1, blocking collectives, body(): projected = jnp.sum(lax.all_gather(mine, 'loop'), axis=0)  15.6 us
    ppermute x3, waiting for transfers between devices, partner(): return lax.ppermute(value, axis, pairs)  12.5 us
    ppermute x2, waiting for transfers between devices, from_behind(): lax.ppermute(shard, axis, [(i, (i + by) % devices) for i in range(devices)])  9.41 us
    ppermute x3, starting transfers between devices, partner(): return lax.ppermute(value, axis, pairs)  5.31 us
    ppermute x2, starting transfers between devices, from_behind(): lax.ppermute(shard, axis, [(i, (i + by) % devices) for i in range(devices)])  3.68 us
    gather x1, local copies, waits for them, and re-layouts, body(): ordered = partial_value[obs_order]  2.31 us
  transfers between devices with their start and end apart: 6, of which 6 were waited for; matrix products, arithmetic and copies ran while one was open for 2% of the time, Pallas kernels for 0%

profile of v1, /device:TPU:0, one launch (start us, length us, event | category | flops | bytes accessed | tf_op | source)
XLA Modules:
  0.0 109.5 jit_solution(15772115874556824561)
XLA Ops:
  7.2 1.8 %fusion.8 = f32[128,512]{1,0:T(8,128)S(1)} fusion(bf16[1,1024,512]{2,1,0:T(8,128)(2,1)} %param.7, bf16[1,1024,128]{2,1,0:T(8,128)(2,1)} %param.10), kind=kOutput, calls=%fused_computation.12 | convolution fusion | flops 134217728 | bytes 1572864 | tf_op jit(solution)/shard_map/dot_general | solution.py:26
  9.0 0.6 collective-permute-start
  9.6 1.2 %collective-permute-done = f32[128,512]{1,0:T(8,128)S(1)} collective-permute-done((f32[128,512]{1,0:T(8,128)S(1)}, f32[128,512]{1,0:T(8,128)S(1)}, u32[]{:S(2)}, u32[]{:S(2)}) %collective-permute-start) | collective-permute-done | bytes 262176 | tf_op jit(solution)/shard_map/ppermute | solution.py:10
  10.8 2.9 %collective-permute-start.1 = (f32[128,512]{1,0:T(8,128)S(1)}, f32[128,512]{1,0:T(8,128)S(1)}, u32[]{:S(2)}, u32[]{:S(2)}) collective-permute-start(f32[128,512]{1,0:T(8,128)S(1)} %add.38), channel_id=1, source_target_pairs={{0,8},{4,12},{8,0},{12,4},{16,24},{20,28},{24,16},{28,20},{1,9},{5... | collective-permute-start | bytes 786440 | tf_op jit(solution)/shard_map/ppermute | solution.py:10
  13.7 6.6 %collective-permute-done.1 = f32[128,512]{1,0:T(8,128)S(1)} collective-permute-done((f32[128,512]{1,0:T(8,128)S(1)}, f32[128,512]{1,0:T(8,128)S(1)}, u32[]{:S(2)}, u32[]{:S(2)}) %collective-permute-start.1) | collective-permute-done | bytes 262176 | tf_op jit(solution)/shard_map/ppermute | solution.py:10
  20.4 1.8 %collective-permute-start.2 = (f32[128,512]{1,0:T(8,128)S(1)}, f32[128,512]{1,0:T(8,128)S(1)}, u32[]{:S(2)}, u32[]{:S(2)}) collective-permute-start(f32[128,512]{1,0:T(8,128)S(1)} %add.40), channel_id=1, source_target_pairs={{0,16},{4,20},{8,24},{12,28},{16,0},{20,4},{24,8},{28,12},{1,17},{... | collective-permute-start | bytes 786440 | tf_op jit(solution)/shard_map/ppermute | solution.py:10
  22.2 1.2 %fusion.1 = f32[1024,512]{1,0:T(8,128)S(1)} fusion(bf16[1,1024,1024]{2,1,0:T(8,128)(2,1)S(1)} %copy-done, bf16[1,1024,512]{2,1,0:T(8,128)(2,1)S(1)} %copy-done.2), kind=kOutput, calls=%fused_computation.3 | convolution fusion | flops 1073741824 | bytes 5242880 | tf_op jit(solution)/shard_map/dot_general | solution.py:41
  23.5 4.7 %collective-permute-done.2 = f32[128,512]{1,0:T(8,128)S(1)} collective-permute-done((f32[128,512]{1,0:T(8,128)S(1)}, f32[128,512]{1,0:T(8,128)S(1)}, u32[]{:S(2)}, u32[]{:S(2)}) %collective-permute-start.2) | collective-permute-done | bytes 262176 | tf_op jit(solution)/shard_map/ppermute | solution.py:10
  28.3 3.6 %collective-permute-start.4 = (f32[128,512]{1,0:T(8,128)S(1)}, f32[128,512]{1,0:T(8,128)S(1)}, u32[]{:S(2)}, u32[]{:S(2)}) collective-permute-start(f32[128,512]{1,0:T(8,128)S(1)} %add.42), channel_id=1, source_target_pairs={{0,3},{1,0},{2,1},{3,2},{4,7},{5,4},{6,5},{7,6},{8,11},{9,8},{10,9... | collective-permute-start | bytes 786440 | tf_op jit(solution)/shard_map/ppermute | solution.py:15
  31.9 0.4 fusion.19
  32.3 0.4 fusion.17
  32.7 5.8 %collective-permute-done.4 = f32[128,512]{1,0:T(8,128)S(1)} collective-permute-done((f32[128,512]{1,0:T(8,128)S(1)}, f32[128,512]{1,0:T(8,128)S(1)}, u32[]{:S(2)}, u32[]{:S(2)}) %collective-permute-start.4) | collective-permute-done | bytes 262176 | tf_op jit(solution)/shard_map/ppermute | solution.py:15
  38.6 0.4 fusion.13
  39.0 3.6 %collective-permute-done.3 = f32[128,512]{1,0:T(8,128)S(1)} collective-permute-done((f32[128,512]{1,0:T(8,128)S(1)}, f32[128,512]{1,0:T(8,128)S(1)}, u32[]{:S(2)}, u32[]{:S(2)}) %collective-permute-start.3) | collective-permute-done | bytes 262176 | tf_op jit(solution)/shard_map/ppermute | solution.py:15
  42.6 0.4 fusion.15
  43.0 0.4 fusion.6
  43.4 0.4 fusion
  43.8 1.0 copy-done.1
  44.8 1.7 %convolution_bitcast_fusion = f32[512,512]{0,1:T(8,128)} fusion(bf16[1024,512]{1,0:T(8,128)(2,1)S(1)} %fusion, bf16[1,1024,512]{2,1,0:T(8,128)(2,1)S(1)} %copy-done.2), kind=kOutput, calls=%fused_computation.5 | convolution fusion | flops 536870912 | bytes 3145728 | tf_op jit(solution)/shard_map/dot_general | solution.py:44
  46.5 1.6 %copy.10 = f32[512,512]{1,0:T(8,128)S(1)} copy(f32[512,512]{0,1:T(8,128)} %convolution_bitcast_fusion) | data formatting | bytes 2097152 | tf_op jit(solution)/shard_map/dot_general | solution.py:44
  48.0 2.3 %gather_fusion = f32[512,512]{1,0:T(8,128)} fusion(f32[512,512]{1,0:T(8,128)S(1)} %copy.10, s32[1024]{0:T(1024)S(1)} %pad_clamp_fusion), kind=kCustom, calls=%fused_computation | custom fusion | bytes 2099200 | tf_op jit(solution)/shard_map/gather | solution.py:47
  50.4 36.0 %reduce-scatter.2.cloned.1.call-done = f32[64,512]{1,0:T(8,128)} async-done(((f32[512,512]{1,0:T(8,128)}), f32[64,512]{1,0:T(8,128)}) %reduce-scatter.2.cloned.1.call-update) | async-done | bytes 131088 | tf_op jit(solution)/shard_map/reduce_scatter | solution.py:48
  86.3 15.6 %all-gather = f32[256,512]{1,0:T(8,128)S(1)} all-gather(f32[64,512]{1,0:T(8,128)} %reduce-scatter.2.cloned.1.call-done), channel_id=2, replica_groups=mesh['leaf'=8,'loop'=4] {'loop'}, dimensions={0}, use_global_device_ids=true | all-gather | bytes 655360 | tf_op jit(solution)/shard_map/all_gather | solution.py:49
  101.9 0.7 reduce_sum.9
  (21 shorter events, 0.3 us)
Async XLA Ops:
  7.2 15.1 %copy-start = (bf16[1,1024,1024]{2,1,0:T(8,128)(2,1)S(1)}, bf16[1,1024,1024]{2,1,0:T(8,128)(2,1)}, u32[]{:S(2)}) copy-start(bf16[1,1024,1024]{2,1,0:T(8,128)(2,1)} %param.8) | copy-start | bytes 6291460
  7.2 15.0 %copy-start.2 = (bf16[1,1024,512]{2,1,0:T(8,128)(2,1)S(1)}, bf16[1,1024,512]{2,1,0:T(8,128)(2,1)}, u32[]{:S(2)}) copy-start(bf16[1,1024,512]{2,1,0:T(8,128)(2,1)} %param.7) | copy-start | bytes 3145732
  7.2 6.5 %copy-start.6 = (s32[512]{0:T(512)S(1)}, s32[512]{0:T(512)}, u32[]{:S(2)}) copy-start(s32[512]{0:T(512)} %param.13) | copy-start | bytes 6148
  7.2 79.1 %reduce-scatter.2.cloned.1.call-start = ((), (), s32[]{:S(2)}) async-start(), calls=%async_computation.1 | async-start | bytes 1179648 | tf_op jit(solution)/shard_map/reduce_scatter | solution.py:48
  9.0 1.7 %collective-permute-start = (f32[128,512]{1,0:T(8,128)S(1)}, f32[128,512]{1,0:T(8,128)S(1)}, u32[]{:S(2)}, u32[]{:S(2)}) collective-permute-start(f32[128,512]{1,0:T(8,128)S(1)} %fusion.8), channel_id=1, source_target_pairs={{0,4},{4,0},{8,12},{12,8},{16,20},{20,16},{24,28},{28,24},{1,5},{5... | collective-permute-start | bytes 786440 | tf_op jit(solution)/shard_map/ppermute | solution.py:10
  10.8 9.5 %collective-permute-start.1 = (f32[128,512]{1,0:T(8,128)S(1)}, f32[128,512]{1,0:T(8,128)S(1)}, u32[]{:S(2)}, u32[]{:S(2)}) collective-permute-start(f32[128,512]{1,0:T(8,128)S(1)} %add.38), channel_id=1, source_target_pairs={{0,8},{4,12},{8,0},{12,4},{16,24},{20,28},{24,16},{28,20},{1,9},{5... | collective-permute-start | bytes 786440 | tf_op jit(solution)/shard_map/ppermute | solution.py:10
  20.4 11.5 %copy-start.4 = (bf16[1,3,128,128]{3,2,1,0:T(8,128)(2,1)S(1)}, bf16[1,3,128,128]{3,2,1,0:T(8,128)(2,1)}, u32[]{:S(2)}) copy-start(bf16[1,3,128,128]{3,2,1,0:T(8,128)(2,1)} %param.11) | copy-start | bytes 294916
  20.4 18.2 %copy-start.5 = (bf16[1,2,128,128]{3,2,1,0:T(8,128)(2,1)S(1)}, bf16[1,2,128,128]{3,2,1,0:T(8,128)(2,1)}, u32[]{:S(2)}) copy-start(bf16[1,2,128,128]{3,2,1,0:T(8,128)(2,1)} %param.12) | copy-start | bytes 196612
  20.4 7.8 %collective-permute-start.2 = (f32[128,512]{1,0:T(8,128)S(1)}, f32[128,512]{1,0:T(8,128)S(1)}, u32[]{:S(2)}, u32[]{:S(2)}) collective-permute-start(f32[128,512]{1,0:T(8,128)S(1)} %add.40), channel_id=1, source_target_pairs={{0,16},{4,20},{8,24},{12,28},{16,0},{20,4},{24,8},{28,12},{1,17},{... | collective-permute-start | bytes 786440 | tf_op jit(solution)/shard_map/ppermute | solution.py:10
  23.5 19.9 %copy-start.3 = (bf16[1,1024,128]{2,1,0:T(8,128)(2,1)S(1)}, bf16[1,1024,128]{2,1,0:T(8,128)(2,1)}, u32[]{:S(2)}) copy-start(bf16[1,1024,128]{2,1,0:T(8,128)(2,1)} %param.9) | copy-start | bytes 786436
  28.3 10.3 %collective-permute-start.4 = (f32[128,512]{1,0:T(8,128)S(1)}, f32[128,512]{1,0:T(8,128)S(1)}, u32[]{:S(2)}, u32[]{:S(2)}) collective-permute-start(f32[128,512]{1,0:T(8,128)S(1)} %add.42), channel_id=1, source_target_pairs={{0,3},{1,0},{2,1},{3,2},{4,7},{5,4},{6,5},{7,6},{8,11},{9,8},{10,9... | collective-permute-start | bytes 786440 | tf_op jit(solution)/shard_map/ppermute | solution.py:15
  32.3 10.3 %collective-permute-start.3 = (f32[128,512]{1,0:T(8,128)S(1)}, f32[128,512]{1,0:T(8,128)S(1)}, u32[]{:S(2)}, u32[]{:S(2)}) collective-permute-start(f32[128,512]{1,0:T(8,128)S(1)} %add.42), channel_id=1, source_target_pairs={{0,1},{1,2},{2,3},{3,0},{4,5},{5,6},{6,7},{7,4},{8,9},{9,10},{10,1... | collective-permute-start | bytes 786440 | tf_op jit(solution)/shard_map/ppermute | solution.py:15
  43.8 1.0 copy-start.1
Sparse Core Ops, SparseCore 0:
  50.5 35.7 reduce-scatter.1
